TPU v7x, 512 devices: a whole 4x4x16 slice. The times are simulated.
512 devices in a mesh: space: 16 (over z), chaos: 32 (over y, x, core).
Axes of the slice: x: 4, y: 4, z: 16, core: 2. Of those that a mesh axis runs over, the one named last changes fastest.
Arguments:
- field: float32 [1792, 32, 8, 128], P('chaos', 'space'), may hold values from -6 to 6
- modes: float32 [21, 32, 8, 128], P(None, 'space'), may hold values from -6 to 6
- send_rows: int32 [32, 256], P('chaos'), may hold values from 0 to 55, as said below
- pick: int32 [1792, 41], P('chaos'), may hold values from 0 to 255
- mode_ids: int32 [1792, 41], P('chaos'), may hold values from 0 to 20
- coef: float32 [1792, 41], P('chaos'), may hold values from -0.15 to 0.15
Outputs:
- first: float32 [1792, 32, 8, 128], P('chaos', 'space')
- second: float32 [1792, 32, 8, 128], P('chaos', 'space')
Inputs may be any that keep to these rules, and one draw needn't show every extreme that they name: `send_rows`: in row e, each block of 8 entries d * 8 to d * 8 + 7 holds different local terms of owner e.
All inputs are finite; a program needn't handle non-finite values.
Results may differ from a plain program's by a relative error of at most 0.000098.
Values sent between devices are 32-bit elements; how exact they have to be, the bound alone decides.
A program may use at most 64 MiB of HBM per device.

v0:
```python
import jax
import jax.numpy as jnp
from jax import lax
from jax.sharding import PartitionSpec as P


def padded_2(cells, sides, width):
    for axis, dim in sides:
        count = lax.axis_size(axis)
        ends = count - 1
        head = lax.slice_in_dim(cells, 0, width, axis=dim)
        tail = lax.slice_in_dim(cells, cells.shape[dim] - width, cells.shape[dim], axis=dim)
        cells = jnp.concatenate(
            [
                lax.ppermute(tail, axis, [(i, (i + 1) % count) for i in range(ends)]),
                cells,
                lax.ppermute(head, axis, [((i + 1) % count, i) for i in range(ends)]),
            ],
            axis=dim,
        )
    return cells


def laplace(padded):
    center = padded[:, 1:-1]
    side = jnp.pad(center, ((0, 0), (0, 0), (1, 1), (1, 1)))
    beside = padded[:, 2:] + padded[:, :-2]
    beside = beside + side[:, :, 2:, 1:-1] + side[:, :, :-2, 1:-1]
    beside = beside + side[:, :, 1:-1, 2:] + side[:, :, 1:-1, :-2]
    return 6.0 * center - beside


def per_device(field, modes, send_rows, pick, mode_ids, coef):
    rows_out = send_rows[0]
    count_modes = modes.shape[0]
    flat_modes = modes.reshape(count_modes, -1)
    own_terms, count_slots = pick.shape
    pool_size = rows_out.shape[0]

    def pool_images(values):
        padded = padded_2(values, (("space", 1),), 1)
        outgoing = jnp.take(padded, rows_out, axis=0)
        pool = lax.all_to_all(outgoing, "chaos", split_axis=0, concat_axis=0, tiled=True)
        stencil = laplace(pool)
        return stencil.reshape(pool_size, -1)

    def apply(values):
        images = pool_images(values)
        place = (pick[:, :, None] == jnp.arange(pool_size, dtype=jnp.int32)[None, None, :]).astype(
            jnp.float32
        )
        place = place * coef[:, :, None]
        which = (
            mode_ids[:, :, None] == jnp.arange(count_modes, dtype=jnp.int32)[None, None, :]
        ).astype(jnp.float32)
        weights = jnp.einsum("isp,isk->ikp", place, which, precision=lax.Precision.HIGHEST)
        mixed = jnp.dot(
            weights.reshape(own_terms * count_modes, pool_size),
            images,
            precision=lax.Precision.HIGHEST,
            preferred_element_type=jnp.float32,
        )
        mixed = mixed.reshape(own_terms, count_modes, -1)
        result = jnp.sum(mixed * flat_modes[None], axis=1)
        return result.reshape(values.shape)

    first = apply(field)
    second = apply(first)
    return (first, second)


def solution(mesh):
    in_specs = (
        P("chaos", "space", None, None),
        P(None, "space", None, None),
        P("chaos", None),
        P("chaos", None),
        P("chaos", None),
        P("chaos", None),
    )
    out_specs = (P("chaos", "space", None, None), P("chaos", "space", None, None))
    return jax.shard_map(
        per_device, mesh=mesh, in_specs=in_specs, out_specs=out_specs, check_vma=False
    )
```

profile of v0, /device:TPU:1, one launch (start us, length us, event | category | flops | bytes accessed | tf_op | source)
XLA Modules:
  0.0 190.1 jit_solution(5379441638180073153)
XLA Ops:
  0.6 1.1 fusion.20
  1.7 4.4 %collective-permute-start = (f32[56,1,8,128]{3,2,1,0:T(8,128)S(1)}, f32[56,1,8,128]{3,2,1,0:T(8,128)S(1)}, u32[]{:S(2)}, u32[]{:S(2)}) collective-permute-start(f32[56,1,8,128]{3,2,1,0:T(8,128)S(1)} %get-tuple-element.5), channel_id=1, source_target_pairs={{0,32},{32,64},{64,96},{96,128},{128,160},{160,192},{192,224},{224... | collective-permute-start | bytes 688136 | tf_op jit(solution)/shard_map/ppermute | solution.py:15
  6.1 1.3 collective-permute-start.1
  9.0 4.0 %collective-permute-done.1 = f32[56,1,8,128]{3,2,1,0:T(8,128)S(1)} collective-permute-done((f32[56,1,8,128]{3,2,1,0:T(8,128)S(1)}, f32[56,1,8,128]{3,2,1,0:T(8,128)S(1)}, u32[]{:S(2)}, u32[]{:S(2)}) %collective-permute-start.1) | collective-permute-done | bytes 229408 | tf_op jit(solution)/shard_map/ppermute | solution.py:17
  13.0 1.1 pad_maximum_fusion
  14.2 3.0 %gather_fusion = f32[256,4,8,128]{3,2,1,0:T(8,128)} fusion(f32[56,4,8,128]{3,2,1,0:T(8,128)S(1)} %pad_maximum_fusion, s32[1024]{0:T(1024)S(1)} %pad_clamp_fusion), kind=kCustom, calls=%fused_computation.clone | custom fusion | bytes 8389632 | tf_op jit(solution)/shard_map/jit(_take)/gather | solution.py:42
  17.2 4.0 %broadcast_select_fusion.1 = f32[256,4,8,128]{3,2,1,0:T(8,128)} fusion(f32[256,4,8,128]{3,2,1,0:T(8,128)} %gather_fusion, pred[256]{0:T(512)(128)(4,1)S(1)} %compare_and_fusion), kind=kLoop, calls=%fused_computation.28 | loop fusion | flops 1048576 | bytes 8388864 | tf_op jit(solution)/shard_map/jit(_take)/select_n | solution.py:42
  21.3 10.4 %all-to-all-start = ((f32[256,4,8,128]{3,2,1,0:T(8,128)}), f32[256,4,8,128]{3,2,1,0:T(8,128)}, u32[]{:S(2)}, u32[]{:S(2)}) async-start(f32[256,4,8,128]{3,2,1,0:T(8,128)} %broadcast_select_fusion.1), calls=%async_computation | async-start | bytes 8388608 | tf_op jit(solution)/shard_map/all_to_all | solution.py:43
  32.1 2.6 %fusion = f32[56,21,256]{2,1,0:T(8,128)} fusion(f32[56,41]{1,0:T(8,128)S(1)} %copy.10, s32[56,41]{1,0:T(8,128)S(1)} %copy.9, s32[56,41]{1,0:T(8,128)S(1)} %copy.8), kind=kOutput, calls=%fused_computation.12 | convolution fusion | flops 149343328 | bytes 1231776 | tf_op jit(solution)/shard_map/isp,isk->ikp/dot_general | solution.py:56
  34.6 47.3 %all-to-all-done = f32[256,4,8,128]{3,2,1,0:T(8,128)} async-done(((f32[256,4,8,128]{3,2,1,0:T(8,128)}), f32[256,4,8,128]{3,2,1,0:T(8,128)}, u32[]{:S(2)}, u32[]{:S(2)}) %all-to-all-start) | async-done | bytes 4194336 | tf_op jit(solution)/shard_map/all_to_all | solution.py:43
  82.0 1.8 slice.76
  83.7 3.4 %fusion.6 = f32[256,2,8,128]{3,2,1,0:T(8,128)S(1)} fusion(f32[256,2,8,128]{3,2,1,0:T(8,128)S(1)} %slice.76, f32[256,4,8,128]{3,2,1,0:T(8,128)} %all-to-all-done), kind=kLoop, calls=%fused_computation.19 | loop fusion | flops 3670016 | bytes 8388608 | tf_op jit(solution)/shard_map/sub | solution.py:30
  87.1 1.5 reshape.59
  88.7 10.4 %multiply_reduce_fusion.1 = f32[56,2048]{1,0:T(8,128)S(1)} fusion(f32[21,2048]{1,0:T(8,128)S(1)} %bitcast.24, f32[256,2048,1]{1,0,2:T(8,128)} %reshape.59, f32[56,21,256]{2,1,0:T(8,128)} %fusion), kind=kOutput, calls=%fused_computation.11 | convolution fusion | flops 7403454464 | bytes 3932160 | tf_op jit(solution)/shard_map/dot_general | solution.py:57
  99.2 3.6 %collective-permute-start.2 = (f32[56,1,8,128]{3,2,1,0:T(8,128)S(1)}, f32[56,1,8,128]{3,2,1,0:T(8,128)S(1)}, u32[]{:S(2)}, u32[]{:S(2)}) collective-permute-start(f32[56,1,8,128]{3,2,1,0:T(8,128)S(1)} %get-tuple-element.3), channel_id=1, source_target_pairs={{0,32},{32,64},{64,96},{96,128},{128,160},{160,192},{192,224},{224... | collective-permute-start | bytes 688136 | tf_op jit(solution)/shard_map/ppermute | solution.py:15
  102.8 1.3 collective-permute-start.3
  104.1 1.6 collective-permute-done.2
  105.7 5.2 %collective-permute-done.3 = f32[56,1,8,128]{3,2,1,0:T(8,128)S(1)} collective-permute-done((f32[56,1,8,128]{3,2,1,0:T(8,128)S(1)}, f32[56,1,8,128]{3,2,1,0:T(8,128)S(1)}, u32[]{:S(2)}, u32[]{:S(2)}) %collective-permute-start.3) | collective-permute-done | bytes 229408 | tf_op jit(solution)/shard_map/ppermute | solution.py:17
  111.0 3.0 %gather_fusion.1 = f32[256,4,8,128]{3,2,1,0:T(8,128)} fusion(f32[56,4,8,128]{3,2,1,0:T(8,128)S(1)} %pad_maximum_fusion.1, s32[1024]{0:T(1024)S(1)} %pad_clamp_fusion), kind=kCustom, calls=%fused_computation.1.clone | custom fusion | bytes 8389632 | tf_op jit(solution)/shard_map/jit(_take)/gather | solution.py:42
  114.0 2.7 %broadcast_select_fusion = f32[256,4,8,128]{3,2,1,0:T(8,128)S(1)} fusion(f32[256,4,8,128]{3,2,1,0:T(8,128)} %gather_fusion.1, pred[256]{0:T(512)(128)(4,1)S(1)} %compare_and_fusion), kind=kLoop, calls=%fused_computation.27 | loop fusion | flops 1048576 | bytes 8388864 | tf_op jit(solution)/shard_map/jit(_take)/select_n | solution.py:42
  116.7 59.2 %all_to_all.10 = f32[256,4,8,128]{3,2,1,0:T(8,128)S(1)} all-to-all(f32[256,4,8,128]{3,2,1,0:T(8,128)S(1)} %broadcast_select_fusion), channel_id=1, replica_groups=mesh['space'=16,'chaos'=32] {'chaos'}, dimensions={0} | all-to-all | bytes 8388608 | tf_op jit(solution)/shard_map/all_to_all | solution.py:43
  176.2 1.1 fusion.11
  177.3 1.5 reshape.60
  178.9 10.4 %multiply_reduce_fusion = f32[56,2048]{1,0:T(8,128)S(1)} fusion(f32[21,2048]{1,0:T(8,128)S(1)} %bitcast.25, f32[256,2048,1]{1,0,2:T(8,128)} %reshape.60, f32[56,21,256]{2,1,0:T(8,128)} %fusion), kind=kOutput, calls=%fused_computation.10 | convolution fusion | flops 7403454464 | bytes 3932160 | tf_op jit(solution)/shard_map/dot_general | solution.py:57
  (24 shorter events, 3.3 us)
Async XLA Ops:
  1.7 7.3 %collective-permute-start = (f32[56,1,8,128]{3,2,1,0:T(8,128)S(1)}, f32[56,1,8,128]{3,2,1,0:T(8,128)S(1)}, u32[]{:S(2)}, u32[]{:S(2)}) collective-permute-start(f32[56,1,8,128]{3,2,1,0:T(8,128)S(1)} %get-tuple-element.5), channel_id=1, source_target_pairs={{0,32},{32,64},{64,96},{96,128},{128,160},{160,192},{192,224},{224... | collective-permute-start | bytes 688136 | tf_op jit(solution)/shard_map/ppermute | solution.py:15
  6.1 6.9 %collective-permute-start.1 = (f32[56,1,8,128]{3,2,1,0:T(8,128)S(1)}, f32[56,1,8,128]{3,2,1,0:T(8,128)S(1)}, u32[]{:S(2)}, u32[]{:S(2)}) collective-permute-start(f32[56,1,8,128]{3,2,1,0:T(8,128)S(1)} %get-tuple-element.6), channel_id=1, source_target_pairs={{32,0},{64,32},{96,64},{128,96},{160,128},{192,160},{224,192},{256... | collective-permute-start | bytes 688136 | tf_op jit(solution)/shard_map/ppermute | solution.py:17
  21.2 10.5 %copy-start.2 = (s32[56,41]{0,1:T(8,128)S(1)}, s32[56,41]{0,1:T(8,128)}, u32[]{:S(2)}) copy-start(s32[56,41]{0,1:T(8,128)} %param.11) | copy-start | bytes 27556
  21.2 10.5 %copy-start.3 = (s32[56,41]{0,1:T(8,128)S(1)}, s32[56,41]{0,1:T(8,128)}, u32[]{:S(2)}) copy-start(s32[56,41]{0,1:T(8,128)} %param.12) | copy-start | bytes 27556
  21.2 10.6 %copy-start.4 = (f32[56,41]{0,1:T(8,128)S(1)}, f32[56,41]{0,1:T(8,128)}, u32[]{:S(2)}) copy-start(f32[56,41]{0,1:T(8,128)} %param.13) | copy-start | bytes 27556
  21.2 10.7 %copy-start.1 = (f32[21,2,8,128]{3,2,1,0:T(8,128)S(1)}, f32[21,2,8,128]{3,2,1,0:T(8,128)}, u32[]{:S(2)}) copy-start(f32[21,2,8,128]{3,2,1,0:T(8,128)} %param.9) | copy-start | bytes 516100
  21.3 60.7 %all-to-all-start = ((f32[256,4,8,128]{3,2,1,0:T(8,128)}), f32[256,4,8,128]{3,2,1,0:T(8,128)}, u32[]{:S(2)}, u32[]{:S(2)}) async-start(f32[256,4,8,128]{3,2,1,0:T(8,128)} %broadcast_select_fusion.1), calls=%async_computation | async-start | bytes 8388608 | tf_op jit(solution)/shard_map/all_to_all | solution.py:43
  99.2 14.8 %copy-start = (f32[7,8,16,128]{3,2,1,0:T(8,128)}, f32[7,8,16,128]{3,2,1,0:T(8,128)S(1)}, u32[]{:S(2)}) copy-start(f32[7,8,16,128]{3,2,1,0:T(8,128)S(1)} %copy.14) | copy-start | bytes 1376260
  99.2 6.5 %collective-permute-start.2 = (f32[56,1,8,128]{3,2,1,0:T(8,128)S(1)}, f32[56,1,8,128]{3,2,1,0:T(8,128)S(1)}, u32[]{:S(2)}, u32[]{:S(2)}) collective-permute-start(f32[56,1,8,128]{3,2,1,0:T(8,128)S(1)} %get-tuple-element.3), channel_id=1, source_target_pairs={{0,32},{32,64},{64,96},{96,128},{128,160},{160,192},{192,224},{224... | collective-permute-start | bytes 688136 | tf_op jit(solution)/shard_map/ppermute | solution.py:15
  102.8 8.2 %collective-permute-start.3 = (f32[56,1,8,128]{3,2,1,0:T(8,128)S(1)}, f32[56,1,8,128]{3,2,1,0:T(8,128)S(1)}, u32[]{:S(2)}, u32[]{:S(2)}) collective-permute-start(f32[56,1,8,128]{3,2,1,0:T(8,128)S(1)} %get-tuple-element.4), channel_id=1, source_target_pairs={{32,0},{64,32},{96,64},{128,96},{160,128},{192,160},{224,192},{256... | collective-permute-start | bytes 688136 | tf_op jit(solution)/shard_map/ppermute | solution.py:17
where the time goes:
time: 191 us; the launch traced here: 190 us
  blocking collectives  59.2 us (31%)
  waiting for transfers between devices  58.4 us (31%)
  matrix products  23.3 us (12%)
  starting transfers between devices  21 us (11%)
  other arithmetic  13.9 us (7%)
  local copies, waits for them, and re-layouts  13.5 us (7%)
    all_to_all x1, blocking collectives, pool_images(): lax.all_to_all(outgoing, 'chaos', split_axis=0, concat_axis=0, tiled=True)  59.2 us
    all_to_all x1, waiting for transfers between devices, pool_images(): lax.all_to_all(outgoing, 'chaos', split_axis=0, concat_axis=0, tiled=True)  47.3 us
    dot_general x2, matrix products, apply(): jnp.dot(weights.reshape(own_terms * count_modes, pool_size), images, prec...  20.8 us
    all_to_all x1, starting transfers between devices, pool_images(): lax.all_to_all(outgoing, 'chaos', split_axis=0, concat_axis=0, tiled=True)  10.4 us
    ppermute x2, waiting for transfers between devices, padded_2(): lax.ppermute(head, axis, [((i + 1) % count, i) for i in range(ends)])  9.22 us
    ppermute x2, starting transfers between devices, padded_2(): lax.ppermute(tail, axis, [(i, (i + 1) % count) for i in range(ends)])  7.94 us
    select_n x3, other arithmetic, pool_images(): outgoing = jnp.take(padded, rows_out, axis=0)  7.43 us
    gather x2, local copies, waits for them, and re-layouts, pool_images(): outgoing = jnp.take(padded, rows_out, axis=0)  6.02 us
  transfers between devices with their start and end apart: 5, of which 5 were waited for; matrix products, arithmetic and copies ran while one was open for 2% of the time, Pallas kernels for 0%

commit v1 on v0

v1 whole, which is shorter than its diff:
```python
import functools

import jax
import jax.numpy as jnp
from jax import lax
from jax.experimental import pallas as pl
from jax.experimental.pallas import tpu as pltpu
from jax.sharding import PartitionSpec as P

f32 = jnp.float32
bf16 = jnp.bfloat16
MESH = pl.DeviceIdType.MESH

SPACE = 16
OWNERS = 32
SIDE = 4
TERMS = 56
CAP = 8
POOL = OWNERS * CAP
SLOTS = 41
MODES = 21
MODES_PAD = 24
PLANES = 2
GX = 8
GY = 128
CELL_ROWS = GX * PLANES
W_ROWS = 1184
AWAY = OWNERS - 1

FIRST_STEPS = ((0, 4), (4, 8))
SECOND_STEPS = ((0, 3), (3, 6), (6, 8))
HALO_STEPS = ((0, 4), (4, 8))


def _offsets():
    far = lambda n: min(n, SIDE - n)
    every = [
        (dy, dx, dc)
        for dy in range(SIDE)
        for dx in range(SIDE)
        for dc in range(2)
        if (dy, dx, dc) != (0, 0, 0)
    ]
    return sorted(every, key=lambda t: -(far(t[0]) + far(t[1])))


def _lanes(values):
    lane = lax.broadcasted_iota(jnp.int32, values.shape, 1)
    after = jnp.where(lane == GY - 1, 0.0, pltpu.roll(values, GY - 1, axis=1))
    before = jnp.where(lane == 0, 0.0, pltpu.roll(values, 1, axis=1))
    return after + before


def _laplace(lo, hi, low_ref, high_ref, has_low, has_high, terms, lap):
    for g in range(lo, hi):
        for p in range(PLANES):
            center = terms[g, p]
            if p == 0:
                outer = jnp.where(has_low, low_ref[g], 0.0)
            else:
                outer = jnp.where(has_high, high_ref[g], 0.0)
            beside = terms[g, 1 - p] + outer + _lanes(center)
            if g > 0:
                beside = beside + terms[g - 1, p]
            if g < GX - 1:
                beside = beside + terms[g + 1, p]
            lap[pl.ds((g * PLANES + p) * TERMS, TERMS), :] = 6.0 * center - beside


def _weights(pick_ref, mid_ref, coef_ref, wf, wcat):
    def row(i, carry):
        picked = pick_ref[pl.ds(i, 1), :]
        mode = mid_ref[pl.ds(i, 1), :]
        coef = coef_ref[pl.ds(i, 1), :]
        which = jnp.where(
            lax.broadcasted_iota(jnp.int32, (MODES_PAD, SLOTS), 0) == mode, coef, 0.0
        )
        place = jnp.where(
            lax.broadcasted_iota(jnp.int32, (POOL, SLOTS), 0) == picked, 1.0, 0.0
        ).astype(bf16)
        top = which.astype(bf16)
        rest = which - top.astype(f32)
        mid = rest.astype(bf16)
        low = (rest - mid.astype(f32)).astype(bf16)
        parts = lax.dot_general(
            jnp.concatenate([top, mid, low], axis=0),
            place,
            (((1,), (1,)), ((), ())),
            preferred_element_type=f32,
        )
        n = MODES_PAD
        total = parts[0:n] + (parts[n : 2 * n] + parts[2 * n : 3 * n])
        wf[0, pl.ds(i, n, stride=TERMS), :] = total[:, 0:128]
        wf[1, pl.ds(i, n, stride=TERMS), :] = total[:, 128:256]
        return carry

    lax.fori_loop(0, TERMS, row, 0)

    def split(t, carry):
        at = pl.multiple_of(t * 16, 16)
        for h in range(2):
            w = wf[h, pl.ds(at, 16), :]
            top = w.astype(bf16)
            low = (w - top.astype(f32)).astype(bf16)
            wcat[pl.ds(at, 16), h * 128 : (h + 1) * 128] = top
            wcat[pl.ds(at, 16), POOL + h * 128 : POOL + (h + 1) * 128] = top
            wcat[pl.ds(at, 16), 2 * POOL + h * 128 : 2 * POOL + (h + 1) * 128] = low
        return carry

    lax.fori_loop(0, W_ROWS // 16, split, 0)


def _mix(lo, hi, pool, wcat, modes, mixed, out, terms):
    def one(g, carry):
        images = jnp.concatenate(
            [
                pool[pl.ds(pl.multiple_of(g * PLANES * POOL, POOL), POOL), :],
                pool[pl.ds(pl.multiple_of(g * PLANES * POOL + POOL, POOL), POOL), :],
            ],
            axis=1,
        )
        top = images.astype(bf16)
        low = (images - top.astype(f32)).astype(bf16)
        mixed[...] = jnp.dot(
            wcat[...], jnp.concatenate([top, low, top], axis=0), preferred_element_type=f32
        )
        for p in range(PLANES):
            total = None
            for k in range(MODES):
                scale = modes[pl.ds(k * CELL_ROWS + p * GX + g, 1), :]
                part = mixed[k * TERMS : (k + 1) * TERMS, p * GY : (p + 1) * GY] * scale
                total = part if total is None else total + part
            out[pl.ds(p * GX + g, TERMS, stride=CELL_ROWS), :] = total
            if terms is not None:
                terms[g, p] = total
        return carry

    lax.fori_loop(lo, hi, one, 0)


def _kernel(
    field_hbm, modes_ref, rows_ref, pick_ref, mid_ref, coef_ref,
    first_hbm, second_hbm,
    field, terms_a, terms_b, low_a, low_b, high_a, high_b, lap,
    stage_a, stage_b, pool_a, pool_b, wf, wcat, mixed, out_a, out_b,
    local_sem, halo_send, halo_recv, send_sem, recv_sem,
):
    z = lax.axis_index("space")
    me = lax.axis_index("chaos")
    core = me % 2
    x = (me // 2) % SIDE
    y = me // (2 * SIDE)
    above = (z + 1) % SPACE
    below = (z + SPACE - 1) % SPACE
    has_low = z > 0
    has_high = z < SPACE - 1

    load = pltpu.make_async_copy(field_hbm, field, local_sem.at[0])
    load.start()

    peers = [
        (((y + dy) % SIDE) * SIDE + (x + dx) % SIDE) * 2 + (core + dc) % 2
        for dy, dx, dc in _offsets()
    ]
    barrier = pltpu.get_barrier_semaphore()
    for near in (above, below):
        pl.semaphore_signal(barrier, inc=1, device_id={"space": near}, device_id_type=MESH)
    for peer in peers:
        pl.semaphore_signal(barrier, inc=1, device_id={"chaos": peer}, device_id_type=MESH)

    load.wait()
    for g in range(GX):
        for p in range(PLANES):
            terms_a[g, p] = field[pl.ds(p * GX + g, TERMS, stride=CELL_ROWS), :]

    pl.semaphore_wait(barrier, AWAY + 2)

    def halo(apply, step, terms, low, high):
        lo, hi = HALO_STEPS[step]
        rows = pl.ds(lo, hi - lo)
        up = pltpu.make_async_remote_copy(
            src_ref=terms.at[rows, 1],
            dst_ref=low.at[rows],
            send_sem=halo_send.at[apply, step, 0],
            recv_sem=halo_recv.at[apply, step, 0],
            device_id={"space": above},
            device_id_type=MESH,
        )
        down = pltpu.make_async_remote_copy(
            src_ref=terms.at[rows, 0],
            dst_ref=high.at[rows],
            send_sem=halo_send.at[apply, step, 1],
            recv_sem=halo_recv.at[apply, step, 1],
            device_id={"space": below},
            device_id_type=MESH,
        )
        return up, down

    def exchange(slot, lo, hi, stage, pool):
        first_row, count = lo * PLANES, (hi - lo) * PLANES
        stage3 = stage.reshape(CELL_ROWS, POOL, GY)
        pool3 = pool.reshape(CELL_ROWS, POOL, GY)

        def entry(owner, c):
            term = rows_ref[0, owner * CAP + c]
            return lap[pl.ds(first_row * TERMS + term, count, stride=TERMS), :]

        for peer in peers:
            for c in range(CAP):
                at = first_row * POOL + peer * CAP + c
                stage[pl.ds(at, count, stride=POOL), :] = entry(peer, c)
            pltpu.make_async_remote_copy(
                src_ref=stage3.at[pl.ds(first_row, count), pl.ds(peer * CAP, CAP)],
                dst_ref=pool3.at[pl.ds(first_row, count), pl.ds(me * CAP, CAP)],
                send_sem=send_sem.at[slot],
                recv_sem=recv_sem.at[slot],
                device_id={"chaos": peer},
                device_id_type=MESH,
            ).start()
        for c in range(CAP):
            at = first_row * POOL + me * CAP + c
            pool[pl.ds(at, count, stride=POOL), :] = entry(me, c)

    def settle(slot, lo, hi, buffer, sem):
        part = buffer.reshape(CELL_ROWS, POOL, GY).at[
            pl.ds(lo * PLANES, (hi - lo) * PLANES), pl.ds(0, AWAY * CAP)
        ]
        pltpu.make_async_copy(part, part, sem.at[slot]).wait()

    halos = [halo(0, s, terms_a, low_a, high_a) for s in range(len(HALO_STEPS))]
    for pair in halos:
        for copy in pair:
            copy.start()
    for step, (lo, hi) in enumerate(FIRST_STEPS):
        for copy in halos[step]:
            copy.wait_recv()
        _laplace(lo, hi, low_a, high_a, has_low, has_high, terms_a, lap)
        exchange(step, lo, hi, stage_a, pool_a)

    _weights(pick_ref, mid_ref, coef_ref, wf, wcat)

    later = [halo(1, s, terms_b, low_b, high_b) for s in range(len(HALO_STEPS))]
    todo = list(enumerate(SECOND_STEPS, len(FIRST_STEPS)))
    for step, (lo, hi) in enumerate(FIRST_STEPS):
        settle(step, lo, hi, pool_a, recv_sem)
        _mix(lo, hi, pool_a, wcat, modes_ref, mixed, out_a, terms_b)
        for copy in later[step]:
            copy.start()
        for copy in later[step]:
            copy.wait_recv()
        ready = hi if hi == GX else hi - 1
        while todo and todo[0][1][1] <= ready:
            slot, (start, stop) = todo.pop(0)
            _laplace(start, stop, low_b, high_b, has_low, has_high, terms_b, lap)
            exchange(slot, start, stop, stage_b, pool_b)

    save_a = pltpu.make_async_copy(out_a, first_hbm, local_sem.at[1])
    save_a.start()
    for slot, (lo, hi) in enumerate(SECOND_STEPS, len(FIRST_STEPS)):
        settle(slot, lo, hi, pool_b, recv_sem)
        _mix(lo, hi, pool_b, wcat, modes_ref, mixed, out_b, None)
    save_b = pltpu.make_async_copy(out_b, second_hbm, local_sem.at[0])
    save_b.start()

    for step, (lo, hi) in enumerate(FIRST_STEPS):
        settle(step, lo, hi, stage_a, send_sem)
    for slot, (lo, hi) in enumerate(SECOND_STEPS, len(FIRST_STEPS)):
        settle(slot, lo, hi, stage_b, send_sem)
    for pair in halos + later:
        for copy in pair:
            copy.wait_send()
    save_a.wait()
    save_b.wait()


def per_device(field, modes, send_rows, pick, mode_ids, coef):
    flat = jax.ShapeDtypeStruct((TERMS * CELL_ROWS, GY), f32)
    vmem = pl.BlockSpec(memory_space=pltpu.VMEM)
    smem = pl.BlockSpec(memory_space=pltpu.SMEM)
    anywhere = pl.BlockSpec(memory_space=pl.ANY)
    steps = len(FIRST_STEPS) + len(SECOND_STEPS)
    first, second = pl.pallas_call(
        _kernel,
        out_shape=(flat, flat),
        in_specs=[anywhere, vmem, smem, vmem, vmem, vmem],
        out_specs=(anywhere, anywhere),
        name="galerkin",
        scratch_shapes=[
            pltpu.VMEM((TERMS * CELL_ROWS, GY), f32),
            *[pltpu.VMEM((GX, PLANES, TERMS, GY), f32)] * 2,
            *[pltpu.VMEM((GX, TERMS, GY), f32)] * 4,
            pltpu.VMEM((CELL_ROWS * TERMS, GY), f32),
            *[pltpu.VMEM((CELL_ROWS * POOL, GY), f32)] * 4,
            pltpu.VMEM((2, MODES_PAD * TERMS, GY), f32),
            pltpu.VMEM((W_ROWS, 3 * POOL), bf16),
            pltpu.VMEM((W_ROWS, PLANES * GY), f32),
            *[pltpu.VMEM((TERMS * CELL_ROWS, GY), f32)] * 2,
            pltpu.SemaphoreType.DMA((2,)),
            pltpu.SemaphoreType.DMA((2, len(HALO_STEPS), 2)),
            pltpu.SemaphoreType.DMA((2, len(HALO_STEPS), 2)),
            pltpu.SemaphoreType.DMA((steps,)),
            pltpu.SemaphoreType.DMA((steps,)),
        ],
        compiler_params=pltpu.CompilerParams(
            collective_id=0, has_side_effects=True, vmem_limit_bytes=40 << 20
        ),
    )(
        field.reshape(TERMS * CELL_ROWS, GY),
        modes.reshape(MODES * CELL_ROWS, GY),
        send_rows,
        pick,
        mode_ids,
        coef,
    )
    return first.reshape(field.shape), second.reshape(field.shape)


def solution(mesh):
    in_specs = (
        P("chaos", "space", None, None),
        P(None, "space", None, None),
        P("chaos", None),
        P("chaos", None),
        P("chaos", None),
        P("chaos", None),
    )
    out_specs = (P("chaos", "space", None, None), P("chaos", "space", None, None))
    return jax.shard_map(
        per_device, mesh=mesh, in_specs=in_specs, out_specs=out_specs, check_vma=False
    )
```

time: 191 us -> 83.5 us (0.44)
  Pallas kernels: 0 us -> 76.1 us
  blocking collectives: 59.2 us -> 0 us
  waiting for transfers between devices: 58.4 us -> 0 us
  matrix products: 23.3 us -> 0 us
  starting transfers between devices: 21 us -> 0 us
  other arithmetic: 13.9 us -> 0 us
  local copies, waits for them, and re-layouts: 13.5 us -> 5.71 us
    pallas_call x0 -> x1, Pallas kernels: none -> 76.1 us  [per_device(): pl.pallas_call(_kernel, out_shape=(flat, flat), in_specs=[anywhere, vmem,...]
    all_to_all x1 -> x0, blocking collectives: 59.2 us -> none  [pool_images(): lax.all_to_all(outgoing, 'chaos', split_axis=0, concat_axis=0, tiled=True)]
    all_to_all x1 -> x0, waiting for transfers between devices: 47.3 us -> none  [pool_images(): lax.all_to_all(outgoing, 'chaos', split_axis=0, concat_axis=0, tiled=True)]
    dot_general x3 -> x0, matrix products: 23.3 us -> none  [the longest x2 20.8 us: apply(): jnp.dot(weights.reshape(own_terms * count_modes, pool_size), images, prec...]
    ppermute x4 -> x0, waiting for transfers between devices: 11.1 us -> none  [the longest x2 9.22 us: padded_2(): lax.ppermute(head, axis, [((i + 1) % count, i) for i in range(ends)])]
    ppermute x4 -> x0, starting transfers between devices: 10.5 us -> none  [the longest x2 7.94 us: padded_2(): lax.ppermute(tail, axis, [(i, (i + 1) % count) for i in range(ends)])]
    all_to_all x1 -> x0, starting transfers between devices: 10.4 us -> none  [pool_images(): lax.all_to_all(outgoing, 'chaos', split_axis=0, concat_axis=0, tiled=True)]
    select_n x3 -> x0, other arithmetic: 7.43 us -> none  [pool_images(): outgoing = jnp.take(padded, rows_out, axis=0)]
  transfers between devices with their start and end apart: 5 -> 0, of which waited for: 5 -> 0; matrix products, arithmetic and copies ran while one was open for 2% -> 0% of each run, Pallas kernels for 0% -> 0%
where the time goes in v1:
time: 83.5 us; the launch traced here: 82.4 us
  Pallas kernels  76.1 us (91%)
  local copies, waits for them, and re-layouts  5.71 us (7%)
    pallas_call x1, Pallas kernels, per_device(): pl.pallas_call(_kernel, out_shape=(flat, flat), in_specs=[anywhere, vmem,...  76.1 us
    unnamed x15, local copies, waits for them, and re-layouts  5.71 us

profile of v1, /device:TPU:1, one launch (start us, length us, event | category | flops | bytes accessed | tf_op | source)
XLA Modules:
  0.0 82.4 jit_solution(15875612792487334890)
XLA Ops:
  0.6 0.0 copy-start.3
  0.6 0.8 copy.8.pick_ref
  1.5 0.0 copy-done.3
  1.5 0.0 copy-start.4
  1.5 0.1 copy.9.mid_ref
  1.6 0.6 copy-done.4
  2.2 0.0 copy-start.2
  2.2 0.1 copy.10.coef_ref
  2.3 0.6 copy-done.2
  2.9 0.0 copy-start
  2.9 1.0 %copy-done = f32[56,2,8,128]{3,2,1,0:T(8,128)S(1)} copy-done((f32[56,2,8,128]{3,2,1,0:T(8,128)S(1)}, f32[56,2,8,128]{3,2,1,0:T(8,128)}, u32[]{:S(2)}) %copy-start) | copy-done | bytes 458776
  3.9 0.0 copy-start.1
  3.9 0.9 %copy-done.1 = f32[21,2,8,128]{3,2,1,0:T(8,128)S(1)} copy-done((f32[21,2,8,128]{3,2,1,0:T(8,128)S(1)}, f32[21,2,8,128]{3,2,1,0:T(8,128)}, u32[]{:S(2)}) %copy-start.1) | copy-done | bytes 172056
  4.8 76.1 %galerkin.1 = (f32[896,128]{1,0:T(8,128)S(1)}, f32[896,128]{1,0:T(8,128)S(1)}) custom-call(f32[896,128]{1,0:T(8,128)S(1)} %bitcast.6, f32[336,128]{1,0:T(8,128)S(1)} %bitcast.7, s32[1,256]{1,0:T(1,128)S(1)} %copy-done.2, s32[56,41]{1,0:T(8,128)S(1)} %copy.8.pick_ref, s32[56,41]{1,0:T(8,128)S(1)} %copy.9.mid_ref, f32[56,41]{1,0:T(8,128)S(1)} %copy.10.coef_ref), custom_call_target="tpu_custom_call" | custom-call | tf_op jit(solution)/shard_map/galerkin/pallas_call | solution.py:282
  80.9 0.8 copy.13
  81.7 0.8 copy.14
Async XLA Ops:
  0.6 0.8 %copy-start.3 = (s32[56,41]{0,1:T(8,128)S(1)}, s32[56,41]{0,1:T(8,128)}, u32[]{:S(2)}) copy-start(s32[56,41]{0,1:T(8,128)} %param.10) | copy-start | bytes 27556
  1.5 0.7 copy-start.4
  2.2 0.7 copy-start.2
  2.9 1.0 %copy-start = (f32[56,2,8,128]{3,2,1,0:T(8,128)S(1)}, f32[56,2,8,128]{3,2,1,0:T(8,128)}, u32[]{:S(2)}) copy-start(f32[56,2,8,128]{3,2,1,0:T(8,128)} %param.6) | copy-start | bytes 1376260
  3.9 0.9 %copy-start.1 = (f32[21,2,8,128]{3,2,1,0:T(8,128)S(1)}, f32[21,2,8,128]{3,2,1,0:T(8,128)}, u32[]{:S(2)}) copy-start(f32[21,2,8,128]{3,2,1,0:T(8,128)} %param.7) | copy-start | bytes 516100

commit v2 on v1

--- a/solution.py
+++ b/solution.py
@@ -24,12 +24,13 @@
 GX = 8
 GY = 128
 CELL_ROWS = GX * PLANES
+BLOCKS = 3
+GROUP = 19
 W_ROWS = 1184
 AWAY = OWNERS - 1
 
-FIRST_STEPS = ((0, 4), (4, 8))
-SECOND_STEPS = ((0, 3), (3, 6), (6, 8))
-HALO_STEPS = ((0, 4), (4, 8))
+FIRST_STEPS = ((0, 2), (2, 5), (5, 8))
+SECOND_STEPS = ((0, 1), (1, 4), (4, 6), (6, 8))
 
 
 def _offsets():
@@ -51,14 +52,11 @@
     return after + before
 
 
-def _laplace(lo, hi, low_ref, high_ref, has_low, has_high, terms, lap):
+def _laplace(lo, hi, low_ref, high_ref, terms, lap):
     for g in range(lo, hi):
         for p in range(PLANES):
             center = terms[g, p]
-            if p == 0:
-                outer = jnp.where(has_low, low_ref[g], 0.0)
-            else:
-                outer = jnp.where(has_high, high_ref[g], 0.0)
+            outer = (high_ref if p else low_ref)[g]
             beside = terms[g, 1 - p] + outer + _lanes(center)
             if g > 0:
                 beside = beside + terms[g - 1, p]
@@ -68,15 +66,29 @@
 
 
 def _weights(pick_ref, mid_ref, coef_ref, wf, wcat):
-    def row(i, carry):
-        picked = pick_ref[pl.ds(i, 1), :]
-        mode = mid_ref[pl.ds(i, 1), :]
-        coef = coef_ref[pl.ds(i, 1), :]
-        which = jnp.where(
-            lax.broadcasted_iota(jnp.int32, (MODES_PAD, SLOTS), 0) == mode, coef, 0.0
-        )
+    lane = lax.broadcasted_iota(jnp.int32, (1, GY), 1)
+
+    def side_by_side(ref, q, blocks):
+        joined = ref[pl.ds(q, 1), :]
+        for j in range(1, blocks):
+            moved = pltpu.roll(ref[pl.ds(q + j * GROUP, 1), :], j * SLOTS, axis=1)
+            joined = jnp.where(lane < j * SLOTS, joined, moved)
+        return joined
+
+    def rows(q, blocks):
+        picked = side_by_side(pick_ref, q, blocks)
+        mode = side_by_side(mid_ref, q, blocks)
+        coef = side_by_side(coef_ref, q, blocks)
+        n = MODES_PAD
+        which = []
+        for j in range(blocks):
+            mine = (lane >= j * SLOTS) & (lane < (j + 1) * SLOTS)
+            kind = jnp.where(mine, mode, -1)
+            hit = lax.broadcasted_iota(jnp.int32, (n, GY), 0) == kind
+            which.append(jnp.where(hit, coef, 0.0))
+        which = jnp.concatenate(which, axis=0)
         place = jnp.where(
-            lax.broadcasted_iota(jnp.int32, (POOL, SLOTS), 0) == picked, 1.0, 0.0
+            lax.broadcasted_iota(jnp.int32, (POOL, GY), 0) == picked, 1.0, 0.0
         ).astype(bf16)
         top = which.astype(bf16)
         rest = which - top.astype(f32)
@@ -88,13 +100,19 @@
             (((1,), (1,)), ((), ())),
             preferred_element_type=f32,
         )
-        n = MODES_PAD
-        total = parts[0:n] + (parts[n : 2 * n] + parts[2 * n : 3 * n])
-        wf[0, pl.ds(i, n, stride=TERMS), :] = total[:, 0:128]
-        wf[1, pl.ds(i, n, stride=TERMS), :] = total[:, 128:256]
+        m = n * blocks
+        total = parts[0:m] + (parts[m : 2 * m] + parts[2 * m : 3 * m])
+        for j in range(blocks):
+            at = pl.ds(q + j * GROUP, n, stride=TERMS)
+            wf[0, at, :] = total[j * n : (j + 1) * n, 0:128]
+            wf[1, at, :] = total[j * n : (j + 1) * n, 128:256]
+
+    def body(q, carry):
+        rows(q, BLOCKS)
         return carry
 
-    lax.fori_loop(0, TERMS, row, 0)
+    lax.fori_loop(0, GROUP - 1, body, 0)
+    rows(GROUP - 1, BLOCKS - 1)
 
     def split(t, carry):
         at = pl.multiple_of(t * 16, 16)
@@ -110,7 +128,7 @@
     lax.fori_loop(0, W_ROWS // 16, split, 0)
 
 
-def _mix(lo, hi, pool, wcat, modes, mixed, out, terms):
+def _mix(lo, hi, pool, wcat, modes, mixed, out, terms, done=None):
     def one(g, carry):
         images = jnp.concatenate(
             [
@@ -133,15 +151,17 @@
             out[pl.ds(p * GX + g, TERMS, stride=CELL_ROWS), :] = total
             if terms is not None:
                 terms[g, p] = total
+        if done is not None:
+            done(g)
         return carry
 
     lax.fori_loop(lo, hi, one, 0)
 
 
 def _kernel(
-    field_hbm, modes_ref, rows_ref, pick_ref, mid_ref, coef_ref,
+    field_hbm, modes_hbm, rows_hbm, pick_hbm, mid_hbm, coef_hbm,
     first_hbm, second_hbm,
-    field, terms_a, terms_b, low_a, low_b, high_a, high_b, lap,
+    field, modes_ref, rows_ref, pick_t, mid_t, coef_t, pick_ref, mid_ref, coef_ref, terms_a, terms_b, low_a, low_b, high_a, high_b, lap,
     stage_a, stage_b, pool_a, pool_b, wf, wcat, mixed, out_a, out_b,
     local_sem, halo_send, halo_recv, send_sem, recv_sem,
 ):
@@ -155,29 +175,53 @@
     has_low = z > 0
     has_high = z < SPACE - 1
 
-    load = pltpu.make_async_copy(field_hbm, field, local_sem.at[0])
-    load.start()
+    pairs = (
+        (field_hbm, field), (rows_hbm, rows_ref), (modes_hbm, modes_ref),
+        (pick_hbm, pick_t), (mid_hbm, mid_t), (coef_hbm, coef_t),
+    )
+    loads = [
+        pltpu.make_async_copy(source, target, local_sem.at[n])
+        for n, (source, target) in enumerate(pairs)
+    ]
+    loads[0].start()
 
     peers = [
         (((y + dy) % SIDE) * SIDE + (x + dx) % SIDE) * 2 + (core + dc) % 2
         for dy, dx, dc in _offsets()
     ]
     barrier = pltpu.get_barrier_semaphore()
-    for near in (above, below):
-        pl.semaphore_signal(barrier, inc=1, device_id={"space": near}, device_id_type=MESH)
+    for there, near in ((has_high, above), (has_low, below)):
+
+        @pl.when(there)
+        def _():
+            pl.semaphore_signal(barrier, inc=1, device_id={"space": near}, device_id_type=MESH)
+
     for peer in peers:
         pl.semaphore_signal(barrier, inc=1, device_id={"chaos": peer}, device_id_type=MESH)
 
-    load.wait()
+    for load in loads[1:]:
+        load.start()
+
+    @pl.when(z == 0)
+    def _():
+        low_a[...] = jnp.zeros_like(low_a)
+        low_b[...] = jnp.zeros_like(low_b)
+
+    @pl.when(z == SPACE - 1)
+    def _():
+        high_a[...] = jnp.zeros_like(high_a)
+        high_b[...] = jnp.zeros_like(high_b)
+
+    loads[0].wait()
     for g in range(GX):
         for p in range(PLANES):
             terms_a[g, p] = field[pl.ds(p * GX + g, TERMS, stride=CELL_ROWS), :]
 
-    pl.semaphore_wait(barrier, AWAY + 2)
-
-    def halo(apply, step, terms, low, high):
-        lo, hi = HALO_STEPS[step]
-        rows = pl.ds(lo, hi - lo)
+    last = SPACE - 1
+    slabs_beside = (z + last - 1) // last + (2 * last - 1 - z) // last
+    pl.semaphore_wait(barrier, AWAY + slabs_beside)
+
+    def halo(apply, step, terms, low, high, rows):
         up = pltpu.make_async_remote_copy(
             src_ref=terms.at[rows, 1],
             dst_ref=low.at[rows],
@@ -196,6 +240,18 @@
         )
         return up, down
 
+    def halo_start(pair):
+        for there, copy in zip((has_high, has_low), pair):
+            pl.when(there)(copy.start)
+
+    def halo_arrive(pair):
+        for there, copy in zip((has_low, has_high), pair):
+            pl.when(there)(copy.wait_recv)
+
+    def halo_leave(pair):
+        for there, copy in zip((has_high, has_low), pair):
+            pl.when(there)(copy.wait_send)
+
     def exchange(slot, lo, hi, stage, pool):
         first_row, count = lo * PLANES, (hi - lo) * PLANES
         stage3 = stage.reshape(CELL_ROWS, POOL, GY)
@@ -227,39 +283,50 @@
         ]
         pltpu.make_async_copy(part, part, sem.at[slot]).wait()
 
-    halos = [halo(0, s, terms_a, low_a, high_a) for s in range(len(HALO_STEPS))]
+    def all_rows(apply, terms, low, high):
+        return [
+            halo(apply, step, terms, low, high, pl.ds(lo, hi - lo))
+            for step, (lo, hi) in enumerate(FIRST_STEPS)
+        ]
+
+    halos = all_rows(0, terms_a, low_a, high_a)
+    later = all_rows(1, terms_b, low_b, high_b)
     for pair in halos:
-        for copy in pair:
-            copy.start()
+        halo_start(pair)
+    loads[1].wait()
     for step, (lo, hi) in enumerate(FIRST_STEPS):
-        for copy in halos[step]:
-            copy.wait_recv()
-        _laplace(lo, hi, low_a, high_a, has_low, has_high, terms_a, lap)
+        halo_arrive(halos[step])
+        _laplace(lo, hi, low_a, high_a, terms_a, lap)
         exchange(step, lo, hi, stage_a, pool_a)
 
+    for load in loads[2:]:
+        load.wait()
+    for source, target in ((pick_t, pick_ref), (mid_t, mid_ref), (coef_t, coef_ref)):
+        target[...] = jnp.zeros_like(target)
+        target[0:TERMS, 0:SLOTS] = jnp.transpose(source[...])
     _weights(pick_ref, mid_ref, coef_ref, wf, wcat)
 
-    later = [halo(1, s, terms_b, low_b, high_b) for s in range(len(HALO_STEPS))]
     todo = list(enumerate(SECOND_STEPS, len(FIRST_STEPS)))
     for step, (lo, hi) in enumerate(FIRST_STEPS):
         settle(step, lo, hi, pool_a, recv_sem)
-        _mix(lo, hi, pool_a, wcat, modes_ref, mixed, out_a, terms_b)
-        for copy in later[step]:
-            copy.start()
-        for copy in later[step]:
-            copy.wait_recv()
+
+        def row_done(g):
+            halo_start(halo(1, step, terms_b, low_b, high_b, pl.ds(g, 1)))
+
+        _mix(lo, hi, pool_a, wcat, modes_ref, mixed, out_a, terms_b, row_done)
+        halo_arrive(later[step])
         ready = hi if hi == GX else hi - 1
         while todo and todo[0][1][1] <= ready:
             slot, (start, stop) = todo.pop(0)
-            _laplace(start, stop, low_b, high_b, has_low, has_high, terms_b, lap)
+            _laplace(start, stop, low_b, high_b, terms_b, lap)
             exchange(slot, start, stop, stage_b, pool_b)
 
-    save_a = pltpu.make_async_copy(out_a, first_hbm, local_sem.at[1])
+    save_a = pltpu.make_async_copy(out_a, first_hbm, local_sem.at[6])
     save_a.start()
     for slot, (lo, hi) in enumerate(SECOND_STEPS, len(FIRST_STEPS)):
         settle(slot, lo, hi, pool_b, recv_sem)
         _mix(lo, hi, pool_b, wcat, modes_ref, mixed, out_b, None)
-    save_b = pltpu.make_async_copy(out_b, second_hbm, local_sem.at[0])
+    save_b = pltpu.make_async_copy(out_b, second_hbm, local_sem.at[7])
     save_b.start()
 
     for step, (lo, hi) in enumerate(FIRST_STEPS):
@@ -267,26 +334,46 @@
     for slot, (lo, hi) in enumerate(SECOND_STEPS, len(FIRST_STEPS)):
         settle(slot, lo, hi, stage_b, send_sem)
     for pair in halos + later:
-        for copy in pair:
-            copy.wait_send()
+        halo_leave(pair)
     save_a.wait()
     save_b.wait()
 
 
+def _save(first, second, first_out, second_out, held_first, held_second, sems):
+    trips = ((second, held_second, second_out), (first, held_first, first_out))
+    loads = [
+        pltpu.make_async_copy(source, held, sems.at[n])
+        for n, (source, held, _) in enumerate(trips)
+    ]
+    stores = [
+        pltpu.make_async_copy(held, target, sems.at[2 + n])
+        for n, (_, held, target) in enumerate(trips)
+    ]
+    for load in loads:
+        load.start()
+    for load, store in zip(loads, stores):
+        load.wait()
+        store.start()
+    for store in stores:
+        store.wait()
+
+
 def per_device(field, modes, send_rows, pick, mode_ids, coef):
     flat = jax.ShapeDtypeStruct((TERMS * CELL_ROWS, GY), f32)
-    vmem = pl.BlockSpec(memory_space=pltpu.VMEM)
-    smem = pl.BlockSpec(memory_space=pltpu.SMEM)
-    anywhere = pl.BlockSpec(memory_space=pl.ANY)
+    hbm = pl.BlockSpec(memory_space=pltpu.HBM)
     steps = len(FIRST_STEPS) + len(SECOND_STEPS)
     first, second = pl.pallas_call(
         _kernel,
         out_shape=(flat, flat),
-        in_specs=[anywhere, vmem, smem, vmem, vmem, vmem],
-        out_specs=(anywhere, anywhere),
+        in_specs=[hbm] * 6,
+        out_specs=(hbm, hbm),
         name="galerkin",
         scratch_shapes=[
             pltpu.VMEM((TERMS * CELL_ROWS, GY), f32),
+            pltpu.VMEM((MODES * CELL_ROWS, GY), f32),
+            pltpu.SMEM((1, POOL), jnp.int32),
+            *[pltpu.VMEM((SLOTS, TERMS), kind) for kind in (jnp.int32, jnp.int32, f32)],
+            *[pltpu.VMEM((64, GY), kind) for kind in (jnp.int32, jnp.int32, f32)],
             *[pltpu.VMEM((GX, PLANES, TERMS, GY), f32)] * 2,
             *[pltpu.VMEM((GX, TERMS, GY), f32)] * 4,
             pltpu.VMEM((CELL_ROWS * TERMS, GY), f32),
@@ -295,23 +382,35 @@
             pltpu.VMEM((W_ROWS, 3 * POOL), bf16),
             pltpu.VMEM((W_ROWS, PLANES * GY), f32),
             *[pltpu.VMEM((TERMS * CELL_ROWS, GY), f32)] * 2,
-            pltpu.SemaphoreType.DMA((2,)),
-            pltpu.SemaphoreType.DMA((2, len(HALO_STEPS), 2)),
-            pltpu.SemaphoreType.DMA((2, len(HALO_STEPS), 2)),
+            pltpu.SemaphoreType.DMA((8,)),
+            pltpu.SemaphoreType.DMA((2, len(FIRST_STEPS), 2)),
+            pltpu.SemaphoreType.DMA((2, len(FIRST_STEPS), 2)),
             pltpu.SemaphoreType.DMA((steps,)),
             pltpu.SemaphoreType.DMA((steps,)),
         ],
         compiler_params=pltpu.CompilerParams(
-            collective_id=0, has_side_effects=True, vmem_limit_bytes=40 << 20
+            collective_id=0, has_side_effects=True, vmem_limit_bytes=60 << 20
         ),
     )(
         field.reshape(TERMS * CELL_ROWS, GY),
         modes.reshape(MODES * CELL_ROWS, GY),
         send_rows,
-        pick,
-        mode_ids,
-        coef,
+        pick.T,
+        mode_ids.T,
+        coef.T,
     )
+    anywhere = pl.BlockSpec(memory_space=pl.ANY)
+    first, second = pl.pallas_call(
+        _save,
+        out_shape=(flat, flat),
+        in_specs=[anywhere] * 2,
+        out_specs=(anywhere,) * 2,
+        name="save",
+        scratch_shapes=[
+            *[pltpu.VMEM((TERMS * CELL_ROWS, GY), f32)] * 2,
+            pltpu.SemaphoreType.DMA((4,)),
+        ],
+    )(first, second)
     return first.reshape(field.shape), second.reshape(field.shape)
 
 

time: 83.5 us -> 65.8 us (0.79); the launches traced: 82.4 us -> 65.6 us
  Pallas kernels: 76.1 us -> 65 us
  local copies, waits for them, and re-layouts: 5.71 us -> 0 us
    pallas_call x1 -> x2, Pallas kernels: 76.1 us -> 65 us  [the longest x1 63 us: per_device(): pl.pallas_call(_kernel, out_shape=(flat, flat), in_specs=[hbm] * 6, out_s...]
    unnamed x15 -> x0, local copies, waits for them, and re-layouts: 5.71 us -> none
where the time goes in v2:
time: 65.8 us; the launch traced here: 65.6 us
  Pallas kernels  65 us (99%)
    pallas_call x1, Pallas kernels, per_device(): pl.pallas_call(_kernel, out_shape=(flat, flat), in_specs=[hbm] * 6, out_s...  63 us
    pallas_call x1, Pallas kernels, per_device(): pl.pallas_call(_save, out_shape=(flat, flat), in_specs=[anywhere] * 2, ou...  1.97 us

profile of v2, /device:TPU:1, one launch (start us, length us, event | category | flops | bytes accessed | tf_op | source)
XLA Modules:
  0.0 65.6 jit_solution(362821938751389143)
XLA Ops:
  0.6 63.0 %galerkin.1 = (f32[896,128]{1,0:T(8,128)}, f32[896,128]{1,0:T(8,128)}) custom-call(f32[896,128]{1,0:T(8,128)} %bitcast.7, f32[336,128]{1,0:T(8,128)} %bitcast.8, s32[1,256]{1,0:T(1,128)} %rows_hbm.1, s32[41,56]{1,0:T(8,128)} %bitcast.9, s32[41,56]{1,0:T(8,128)} %bitcast.10, f32[41,56]{1,0:T(8,128)} %bitcast.11), custom_call_target="tpu_custom_call" | custom-call | tf_op jit(solution)/shard_map/galerkin/pallas_call | solution.py:365
  63.7 2.0 %save.1 = (f32[896,128]{1,0:T(8,128)}, f32[896,128]{1,0:T(8,128)}) custom-call(f32[896,128]{1,0:T(8,128)} %get-tuple-element.6.first, f32[896,128]{1,0:T(8,128)} %get-tuple-element.7.second), custom_call_target="tpu_custom_call" | custom-call | tf_op jit(solution)/shard_map/save/pallas_call | solution.py:403

commit v3 on v2

--- a/solution.py
+++ b/solution.py
@@ -160,9 +160,9 @@
 
 def _kernel(
     field_hbm, modes_hbm, rows_hbm, pick_hbm, mid_hbm, coef_hbm,
-    first_hbm, second_hbm,
+    out_a, out_b,
     field, modes_ref, rows_ref, pick_t, mid_t, coef_t, pick_ref, mid_ref, coef_ref, terms_a, terms_b, low_a, low_b, high_a, high_b, lap,
-    stage_a, stage_b, pool_a, pool_b, wf, wcat, mixed, out_a, out_b,
+    stage_a, stage_b, pool_a, pool_b, wf, wcat, mixed,
     local_sem, halo_send, halo_recv, send_sem, recv_sem,
 ):
     z = lax.axis_index("space")
@@ -321,52 +321,39 @@
             _laplace(start, stop, low_b, high_b, terms_b, lap)
             exchange(slot, start, stop, stage_b, pool_b)
 
-    save_a = pltpu.make_async_copy(out_a, first_hbm, local_sem.at[6])
-    save_a.start()
     for slot, (lo, hi) in enumerate(SECOND_STEPS, len(FIRST_STEPS)):
         settle(slot, lo, hi, pool_b, recv_sem)
         _mix(lo, hi, pool_b, wcat, modes_ref, mixed, out_b, None)
-    save_b = pltpu.make_async_copy(out_b, second_hbm, local_sem.at[7])
-    save_b.start()
-
     for step, (lo, hi) in enumerate(FIRST_STEPS):
         settle(step, lo, hi, stage_a, send_sem)
     for slot, (lo, hi) in enumerate(SECOND_STEPS, len(FIRST_STEPS)):
         settle(slot, lo, hi, stage_b, send_sem)
     for pair in halos + later:
         halo_leave(pair)
-    save_a.wait()
-    save_b.wait()
-
-
-def _save(first, second, first_out, second_out, held_first, held_second, sems):
-    trips = ((second, held_second, second_out), (first, held_first, first_out))
-    loads = [
-        pltpu.make_async_copy(source, held, sems.at[n])
-        for n, (source, held, _) in enumerate(trips)
+
+
+def _save(first, second, first_out, second_out, sems):
+    copies = [
+        pltpu.make_async_copy(first, first_out, sems.at[0]),
+        pltpu.make_async_copy(second, second_out, sems.at[1]),
     ]
-    stores = [
-        pltpu.make_async_copy(held, target, sems.at[2 + n])
-        for n, (_, held, target) in enumerate(trips)
-    ]
-    for load in loads:
-        load.start()
-    for load, store in zip(loads, stores):
-        load.wait()
-        store.start()
-    for store in stores:
-        store.wait()
+    for copy in copies:
+        copy.start()
+    for copy in copies:
+        copy.wait()
 
 
 def per_device(field, modes, send_rows, pick, mode_ids, coef):
     flat = jax.ShapeDtypeStruct((TERMS * CELL_ROWS, GY), f32)
+    held = pltpu.VMEM((TERMS * CELL_ROWS, GY), f32)
     hbm = pl.BlockSpec(memory_space=pltpu.HBM)
+    vmem = pl.BlockSpec(memory_space=pltpu.VMEM)
     steps = len(FIRST_STEPS) + len(SECOND_STEPS)
     first, second = pl.pallas_call(
         _kernel,
-        out_shape=(flat, flat),
+        out_shape=(held, held),
         in_specs=[hbm] * 6,
-        out_specs=(hbm, hbm),
+        out_specs=(vmem, vmem),
         name="galerkin",
         scratch_shapes=[
             pltpu.VMEM((TERMS * CELL_ROWS, GY), f32),
@@ -381,7 +368,6 @@
             pltpu.VMEM((2, MODES_PAD * TERMS, GY), f32),
             pltpu.VMEM((W_ROWS, 3 * POOL), bf16),
             pltpu.VMEM((W_ROWS, PLANES * GY), f32),
-            *[pltpu.VMEM((TERMS * CELL_ROWS, GY), f32)] * 2,
             pltpu.SemaphoreType.DMA((8,)),
             pltpu.SemaphoreType.DMA((2, len(FIRST_STEPS), 2)),
             pltpu.SemaphoreType.DMA((2, len(FIRST_STEPS), 2)),
@@ -399,18 +385,14 @@
         mode_ids.T,
         coef.T,
     )
-    anywhere = pl.BlockSpec(memory_space=pl.ANY)
     first, second = pl.pallas_call(
         _save,
         out_shape=(flat, flat),
-        in_specs=[anywhere] * 2,
-        out_specs=(anywhere,) * 2,
+        in_specs=[pl.BlockSpec(memory_space=pl.ANY)] * 2,
+        out_specs=(pl.BlockSpec(memory_space=pl.ANY),) * 2,
         name="save",
-        scratch_shapes=[
-            *[pltpu.VMEM((TERMS * CELL_ROWS, GY), f32)] * 2,
-            pltpu.SemaphoreType.DMA((4,)),
-        ],
-    )(first, second)
+        scratch_shapes=[pltpu.SemaphoreType.DMA((2,))],
+    )(*(pltpu.with_memory_space_constraint(part, pltpu.VMEM) for part in (first, second)))
     return first.reshape(field.shape), second.reshape(field.shape)
 
 

time: 65.8 us -> 64 us (0.973)
  Pallas kernels: 65 us -> 63.2 us
    pallas_call x2, Pallas kernels: 65 us -> 63.2 us  [the longest x1 62.3 us: per_device(): pl.pallas_call(_kernel, out_shape=(held, held), in_specs=[hbm] * 6, out_s...]
where the time goes in v3:
time: 64 us; the launch traced here: 63.9 us
  Pallas kernels  63.2 us (99%)
  between operations  0.64 us (1%)
    pallas_call x1, Pallas kernels, per_device(): pl.pallas_call(_kernel, out_shape=(held, held), in_specs=[hbm] * 6, out_s...  62.3 us

profile of v3, /device:TPU:1, one launch (start us, length us, event | category | flops | bytes accessed | tf_op | source)
XLA Modules:
  0.0 63.9 jit_solution(14666604601168485357)
XLA Ops:
  0.6 62.3 %galerkin.1 = (f32[896,128]{1,0:T(8,128)S(1)}, f32[896,128]{1,0:T(8,128)S(1)}) custom-call(f32[896,128]{1,0:T(8,128)} %bitcast.7, f32[336,128]{1,0:T(8,128)} %bitcast.8, s32[1,256]{1,0:T(1,128)} %rows_hbm.1, s32[41,56]{1,0:T(8,128)} %bitcast.9, s32[41,56]{1,0:T(8,128)} %bitcast.10, f32[41,56]{1,0:T(8,128)} %bitcast.11), custom_call_target="tpu_custom_call" | custom-call | tf_op jit(solution)/shard_map/galerkin/pallas_call | solution.py:352
  62.9 0.9 %save.1 = (f32[896,128]{1,0:T(8,128)}, f32[896,128]{1,0:T(8,128)}) custom-call(f32[896,128]{1,0:T(8,128)S(1)} %get-tuple-element.6.first, f32[896,128]{1,0:T(8,128)S(1)} %get-tuple-element.7.second), custom_call_target="tpu_custom_call" | custom-call | tf_op jit(solution)/shard_map/save/pallas_call | solution.py:388

commit v4 on v3

--- a/solution.py
+++ b/solution.py
@@ -25,12 +25,13 @@
 GY = 128
 CELL_ROWS = GX * PLANES
 BLOCKS = 3
+EARLY = 9
 GROUP = 19
 W_ROWS = 1184
 AWAY = OWNERS - 1
 
-FIRST_STEPS = ((0, 2), (2, 5), (5, 8))
-SECOND_STEPS = ((0, 1), (1, 4), (4, 6), (6, 8))
+FIRST_STEPS = ((0, 1), (1, 3), (3, 6), (6, 8))
+SECOND_STEPS = ((0, 2), (2, 5), (5, 7), (7, 8))
 
 
 def _offsets():
@@ -65,7 +66,7 @@
             lap[pl.ds((g * PLANES + p) * TERMS, TERMS), :] = 6.0 * center - beside
 
 
-def _weights(pick_ref, mid_ref, coef_ref, wf, wcat):
+def _weights(pick_ref, mid_ref, coef_ref, wf, start, stop):
     lane = lax.broadcasted_iota(jnp.int32, (1, GY), 1)
 
     def side_by_side(ref, q, blocks):
@@ -111,9 +112,12 @@
         rows(q, BLOCKS)
         return carry
 
-    lax.fori_loop(0, GROUP - 1, body, 0)
-    rows(GROUP - 1, BLOCKS - 1)
-
+    lax.fori_loop(start, min(stop, GROUP - 1), body, 0)
+    if stop == GROUP:
+        rows(GROUP - 1, BLOCKS - 1)
+
+
+def _halves(wf, wcat):
     def split(t, carry):
         at = pl.multiple_of(t * 16, 16)
         for h in range(2):
@@ -293,18 +297,19 @@
     later = all_rows(1, terms_b, low_b, high_b)
     for pair in halos:
         halo_start(pair)
-    loads[1].wait()
+    for load in loads[1:]:
+        load.wait()
+    for source, target in ((pick_t, pick_ref), (mid_t, mid_ref), (coef_t, coef_ref)):
+        target[...] = jnp.zeros_like(target)
+        target[0:TERMS, 0:SLOTS] = jnp.transpose(source[...])
+    _weights(pick_ref, mid_ref, coef_ref, wf, 0, EARLY)
     for step, (lo, hi) in enumerate(FIRST_STEPS):
         halo_arrive(halos[step])
         _laplace(lo, hi, low_a, high_a, terms_a, lap)
         exchange(step, lo, hi, stage_a, pool_a)
 
-    for load in loads[2:]:
-        load.wait()
-    for source, target in ((pick_t, pick_ref), (mid_t, mid_ref), (coef_t, coef_ref)):
-        target[...] = jnp.zeros_like(target)
-        target[0:TERMS, 0:SLOTS] = jnp.transpose(source[...])
-    _weights(pick_ref, mid_ref, coef_ref, wf, wcat)
+    _weights(pick_ref, mid_ref, coef_ref, wf, EARLY, GROUP)
+    _halves(wf, wcat)
 
     todo = list(enumerate(SECOND_STEPS, len(FIRST_STEPS)))
     for step, (lo, hi) in enumerate(FIRST_STEPS):

time: 64 us -> 63.4 us (level)
  no operation moved by 1% of the time
where the time goes in v4:
time: 63.4 us; the launch traced here: 63.2 us
  Pallas kernels  62.6 us (99%)
  between operations  0.64 us (1%)
    pallas_call x1, Pallas kernels, per_device(): pl.pallas_call(_kernel, out_shape=(held, held), in_specs=[hbm] * 6, out_s...  61.6 us

profile of v4, /device:TPU:1, one launch (start us, length us, event | category | flops | bytes accessed | tf_op | source)
XLA Modules:
  0.0 63.2 jit_solution(4923179890534156638)
XLA Ops:
  0.6 61.6 %galerkin.1 = (f32[896,128]{1,0:T(8,128)S(1)}, f32[896,128]{1,0:T(8,128)S(1)}) custom-call(f32[896,128]{1,0:T(8,128)} %bitcast.7, f32[336,128]{1,0:T(8,128)} %bitcast.8, s32[1,256]{1,0:T(1,128)} %rows_hbm.1, s32[41,56]{1,0:T(8,128)} %bitcast.9, s32[41,56]{1,0:T(8,128)} %bitcast.10, f32[41,56]{1,0:T(8,128)} %bitcast.11), custom_call_target="tpu_custom_call" | custom-call | tf_op jit(solution)/shard_map/galerkin/pallas_call | solution.py:357
  62.3 0.9 %save.1 = (f32[896,128]{1,0:T(8,128)}, f32[896,128]{1,0:T(8,128)}) custom-call(f32[896,128]{1,0:T(8,128)S(1)} %get-tuple-element.6.first, f32[896,128]{1,0:T(8,128)S(1)} %get-tuple-element.7.second), custom_call_target="tpu_custom_call" | custom-call | tf_op jit(solution)/shard_map/save/pallas_call | solution.py:393
